TPU v7x, 256 devices: a whole 4x4x8 slice. The times are simulated.
256 devices in a mesh: fsdp: 32 (over z, x_hi, core), tensor: 8 (over x_lo, y).
Axes of the slice: x: 4 (x_hi: 2, x_lo: 2; x = x_hi * 2 + x_lo), y: 4, z: 8, core: 2. Of those that a mesh axis runs over, the one named last changes fastest.
Arguments:
- tokens: bfloat16 [49152, 8192], P(('fsdp', 'tensor'))
- gain: bfloat16 [8192], replicated, may hold values from 0.5 to 1.5
- kv_weight: bfloat16 [8192, 2048], P('fsdp', 'tensor'), may hold values from -0.09375 to 0.09375
- block_mask: int32 [64, 16], P('fsdp', 'tensor'), may hold values from 0 to 1
- cotangent: bfloat16 [49152, 2048], P('fsdp', 'tensor'), may hold values from -0.02734375 to 0.02734375
Outputs:
- projected: bfloat16 [49152, 2048], P('fsdp', 'tensor')
- weight_grad: float32 [8192, 2048], P('fsdp', 'tensor')
All inputs are finite; a program needn't handle non-finite values.
Results may differ from a plain program's by a relative error of at most 0.005.
Values may be sent and summed in bfloat16 or wider, within the bound.
A program may use at most 128 MiB of HBM per device.

v0:
```python
import jax
import jax.numpy as jnp
from jax import lax
from jax.sharding import PartitionSpec as P


def normalize(rows, gain):
    values = rows.astype(jnp.float32)
    square = jnp.mean(values * values, axis=-1, keepdims=True)
    return (values * lax.rsqrt(square + 1e-05) * gain.astype(jnp.float32)).astype(jnp.bfloat16)


def apply_mask(panel, mask):
    rows, cols = panel.shape
    mrows, mcols = mask.shape
    shaped = panel.reshape(mrows, rows // mrows, mcols, cols // mcols)
    kept = shaped * mask[:, None, :, None].astype(panel.dtype)
    return kept.reshape(rows, cols)


def per_device(tokens, gain, kv_weight, block_mask, cotangent):
    group = lax.all_gather(normalize(tokens, gain), "tensor", axis=0, tiled=True)
    columns = group
    total = jnp.dot(
        columns,
        apply_mask(
            lax.all_gather(kv_weight, "fsdp", axis=0, tiled=True),
            lax.all_gather(block_mask, "fsdp", axis=0, tiled=True),
        ),
        preferred_element_type=jnp.float32,
    )
    projected = total.astype(jnp.bfloat16)
    columns = group
    summed = lax.psum_scatter(
        lax.dot_general(
            columns, cotangent, (((0,), (0,)), ((), ())), preferred_element_type=jnp.float32
        ),
        "fsdp",
        scatter_dimension=0,
        tiled=True,
    )
    weight_grad = apply_mask(summed, block_mask)
    return (projected, weight_grad)


def solution(mesh):
    return jax.shard_map(
        per_device,
        mesh=mesh,
        in_specs=(
            P(("fsdp", "tensor"), None),
            P(),
            P("fsdp", "tensor"),
            P("fsdp", "tensor"),
            P("fsdp", "tensor"),
        ),
        out_specs=(P("fsdp", "tensor"), P("fsdp", "tensor")),
        check_vma=False,
    )
```

profile of v0, /device:TPU:8, one launch (start us, length us, event | category | flops | bytes accessed | tf_op | source)
XLA Modules:
  0.0 521.2 jit_solution(9037868814021527761)
XLA Ops:
  7.2 0.0 copy-start
  7.2 0.0 all-gather.4.cloned.1.call-start
  7.2 0.8 convert_element_type.21
  8.0 2.6 fusion
  10.6 4.5 fusion.2
  15.1 0.0 all-gather.4.cloned.1.call-update
  15.1 0.0 all-gather.6.cloned.1.call-start
  15.2 0.7 all-gather.6.cloned.1.call-update
  15.9 0.0 reduce-scatter.2.cloned.1.call-start
  15.9 251.8 %all-gather.4.cloned.1.call-done = bf16[1536,8192]{1,0:T(8,128)(2,1)} async-done(((bf16[192,8192]{1,0:T(8,128)(2,1)}), bf16[1536,8192]{1,0:T(8,128)(2,1)}) %all-gather.4.cloned.1.call-update) | async-done | bytes 25165840 | tf_op jit(solution)/shard_map/all_gather | solution.py:22
  267.7 0.0 copy-done
  267.7 13.9 %fusion.6 = f32[8192,256]{1,0:T(8,128)} fusion(bf16[1536,8192]{1,0:T(8,128)(2,1)} %all-gather.4.cloned.1.call-done, bf16[1536,256]{1,0:T(8,128)(2,1)S(1)} %copy-done), kind=kOutput, calls=%fused_computation.11 | convolution fusion | flops 6442450944 | bytes 34340864 | tf_op jit(solution)/shard_map/dot_general | solution.py:35
  281.7 0.0 copy-start.1
  281.7 0.0 reduce-scatter.2.cloned.1.call-update
  281.7 0.7 copy-done.1
  282.4 42.1 %all-gather = s32[32,2,2]{2,1,0:T(2,128)S(1)} all-gather(s32[1,2,2]{2,1,0:T(2,128)S(1)} %bitcast.19), channel_id=1, replica_groups=mesh['fsdp'=32,'tensor'=8] {'fsdp'}, dimensions={0}, use_global_device_ids=true | all-gather | bytes 528 | tf_op jit(solution)/shard_map/all_gather | solution.py:28
  324.5 0.1 copy.13
  324.6 0.1 copy.16
  324.7 33.6 %all-gather.6.cloned.1.call-done = bf16[8192,256]{1,0:T(8,128)(2,1)} async-done(((bf16[256,256]{1,0:T(8,128)(2,1)}), bf16[8192,256]{1,0:T(8,128)(2,1)}) %all-gather.6.cloned.1.call-update) | async-done | bytes 4194320 | tf_op jit(solution)/shard_map/all_gather | solution.py:27
  358.3 2.2 mul.46
  360.5 13.5 %fusion.5 = bf16[1536,256]{1,0:T(8,128)(2,1)} fusion(bf16[1536,8192]{1,0:T(8,128)(2,1)} %all-gather.4.cloned.1.call-done, bf16[8192,256]{1,0:T(8,128)(2,1)} %all-gather.6.cloned.1.call-done, bf16[1024,8,2,128]{3,2,1,0:T(2,128)(2,1)S(1)} %bitcast.16), kind=kOutput, calls=%fused_computation.8 | convolution fusion | flops 6444941312 | bytes 34340864 | tf_op jit(solution)/shard_map/dot_general | solution.py:24
  374.1 138.8 %reduce-scatter.2.cloned.1.call-done = f32[256,256]{1,0:T(8,128)} async-done(((f32[8192,256]{1,0:T(8,128)}), f32[256,256]{1,0:T(8,128)}) %reduce-scatter.2.cloned.1.call-update) | async-done | bytes 262160 | tf_op jit(solution)/shard_map/reduce_scatter | solution.py:34
  512.9 0.1 mul.49
  513.0 1.7 bitcast_multiply_fusion.4
  (3 shorter events, 0.0 us)
Async XLA Ops:
  7.2 260.6 %copy-start = (bf16[1536,256]{1,0:T(8,128)(2,1)S(1)}, bf16[1536,256]{1,0:T(8,128)(2,1)}, u32[]{:S(2)}) copy-start(bf16[1536,256]{1,0:T(8,128)(2,1)} %param.9) | copy-start | bytes 2359300
  7.2 260.6 %all-gather.4.cloned.1.call-start = ((), (), s32[]{:S(2)}) async-start(), calls=%async_computation.1 | async-start | bytes 28311552 | tf_op jit(solution)/shard_map/all_gather | solution.py:22
  15.1 343.2 %all-gather.6.cloned.1.call-start = ((), (), s32[]{:S(2)}) async-start(), calls=%async_computation.2 | async-start | bytes 4325376 | tf_op jit(solution)/shard_map/all_gather | solution.py:27
  15.9 497.0 %reduce-scatter.2.cloned.1.call-start = ((), (), s32[]{:S(2)}) async-start(), calls=%async_computation.3 | async-start | bytes 8650752 | tf_op jit(solution)/shard_map/reduce_scatter | solution.py:34
  281.7 0.7 copy-start.1
Sparse Core Ops, SparseCore 0:
  15.2 252.4 all-gather.3
  270.5 87.7 all-gather.5
  362.7 150.0 reduce-scatter.1
where the time goes:
time: 521 us
  waiting for transfers between devices  425 us (82%)
  blocking collectives  42.1 us (8%)
  matrix products  27.5 us (5%)
  between operations  13.8 us (3%)
  other arithmetic  9.57 us (2%)
    all_gather x1, waiting for transfers between devices, per_device(): lax.all_gather(normalize(tokens, gain), 'tensor', axis=0, tiled=True)  252 us
    reduce_scatter x1, waiting for transfers between devices, per_device(): lax.psum_scatter(lax.dot_general(columns, cotangent, (((0,), (0,)), ((),...  139 us
    all_gather x1, blocking collectives, per_device(): lax.all_gather(block_mask, 'fsdp', axis=0, tiled=True)  42.1 us
    all_gather x1, waiting for transfers between devices, per_device(): lax.all_gather(kv_weight, 'fsdp', axis=0, tiled=True)  33.6 us
    dot_general x1, matrix products, per_device(): lax.dot_general(columns, cotangent, (((0,), (0,)), ((), ())), preferred_e...  13.9 us
    dot_general x1, matrix products, per_device(): jnp.dot(columns, apply_mask(lax.all_gather(kv_weight, 'fsdp', axis=0, til...  13.5 us
  transfers between devices with their start and end apart: 3, of which 3 were waited for; matrix products, arithmetic and copies ran while one was open for 6% of the time, Pallas kernels for 0%

commit v1 on v0

--- a/solution.py
+++ b/solution.py
@@ -24,7 +24,12 @@
     total = jnp.dot(
         columns,
         apply_mask(
-            lax.all_gather(kv_weight, "fsdp", axis=0, tiled=True),
+            jnp.concatenate(
+                lax.all_to_all(
+                    jnp.stack([kv_weight for _ in range(lax.psum(1, "fsdp"))]), "fsdp", 0, 0
+                ),
+                axis=0,
+            ),
             lax.all_gather(block_mask, "fsdp", axis=0, tiled=True),
         ),
         preferred_element_type=jnp.float32,

time: 521 us -> 478 us (0.917)
  waiting for transfers between devices: 425 us -> 267 us
  blocking collectives: 42.1 us -> 144 us
  starting transfers between devices: 0.12 us -> 10 us
    reduce_scatter x1, waiting for transfers between devices: 139 us -> 14.6 us  [per_device(): lax.psum_scatter(lax.dot_general(columns, cotangent, (((0,), (0,)), ((),...]
    all_gather x1, blocking collectives: 42.1 us -> 144 us  [per_device(): lax.all_gather(block_mask, 'fsdp', axis=0, tiled=True)]
    all_gather x1 -> x0, waiting for transfers between devices: 33.6 us -> none  [per_device(): lax.all_gather(kv_weight, 'fsdp', axis=0, tiled=True)]
    all_to_all x0 -> x1, starting transfers between devices: none -> 9.95 us  [per_device(): lax.all_to_all(jnp.stack([kv_weight for _ in range(lax.psum(1, 'fsdp'))])...]
  transfers between devices with their start and end apart: 3 -> 3, of which waited for: 3 -> 2; matrix products, arithmetic and copies ran while one was open for 6% -> 4% of each run, Pallas kernels for 0% -> 0%
where the time goes in v1:
time: 478 us
  waiting for transfers between devices  267 us (56%)
  blocking collectives  144 us (30%)
  matrix products  27.5 us (6%)
  between operations  14.1 us (3%)
  starting transfers between devices  10 us (2%)
  other arithmetic  9.57 us (2%)
  local copies, waits for them, and re-layouts  5.88 us (1%)
    all_gather x1, waiting for transfers between devices, per_device(): lax.all_gather(normalize(tokens, gain), 'tensor', axis=0, tiled=True)  253 us
    all_gather x1, blocking collectives, per_device(): lax.all_gather(block_mask, 'fsdp', axis=0, tiled=True)  144 us
    reduce_scatter x1, waiting for transfers between devices, per_device(): lax.psum_scatter(lax.dot_general(columns, cotangent, (((0,), (0,)), ((),...  14.6 us
    dot_general x1, matrix products, per_device(): lax.dot_general(columns, cotangent, (((0,), (0,)), ((), ())), preferred_e...  13.9 us
    dot_general x1, matrix products, per_device(): jnp.dot(columns, apply_mask(jnp.concatenate(lax.all_to_all(jnp.stack([kv_...  13.6 us
    all_to_all x1, starting transfers between devices, per_device(): lax.all_to_all(jnp.stack([kv_weight for _ in range(lax.psum(1, 'fsdp'))])...  9.95 us
  transfers between devices with their start and end apart: 3, of which 2 were waited for; matrix products, arithmetic and copies ran while one was open for 4% of the time, Pallas kernels for 0%

profile of v1, /device:TPU:8, one launch (start us, length us, event | category | flops | bytes accessed | tf_op | source)
XLA Modules:
  0.0 478.1 jit_solution(15599427118751205558)
XLA Ops:
  7.2 0.0 copy-start
  7.2 0.0 all-gather.3.cloned.1.call-start
  7.2 0.8 convert_element_type.21
  8.0 2.6 fusion
  10.6 4.5 fusion.2
  15.1 0.0 all-gather.3.cloned.1.call-update
  15.1 0.0 reduce-scatter.2.cloned.1.call-start
  15.2 252.6 %all-gather.3.cloned.1.call-done = bf16[1536,8192]{1,0:T(8,128)(2,1)} async-done(((bf16[192,8192]{1,0:T(8,128)(2,1)}), bf16[1536,8192]{1,0:T(8,128)(2,1)}) %all-gather.3.cloned.1.call-update) | async-done | bytes 25165840 | tf_op jit(solution)/shard_map/all_gather | solution.py:22
  267.7 0.0 copy-done
  267.7 13.9 %fusion.6 = f32[8192,256]{1,0:T(8,128)} fusion(bf16[1536,8192]{1,0:T(8,128)(2,1)} %all-gather.3.cloned.1.call-done, bf16[1536,256]{1,0:T(8,128)(2,1)S(1)} %copy-done), kind=kOutput, calls=%fused_computation.11 | convolution fusion | flops 6442450944 | bytes 34340864 | tf_op jit(solution)/shard_map/dot_general | solution.py:40
  281.7 0.0 copy-start.1
  281.7 0.0 reduce-scatter.2.cloned.1.call-update
  281.7 0.9 copy-done.1
  282.6 0.0 copy-start.2
  282.6 2.4 stack.2
  285.0 9.9 %all-to-all-start = ((bf16[32,256,256]{2,1,0:T(8,128)(2,1)}), bf16[32,256,256]{2,1,0:T(8,128)(2,1)}, u32[]{:S(2)}, u32[]{:S(2)}) async-start(bf16[32,256,256]{2,1,0:T(8,128)(2,1)} %stack.2), calls=%async_computation | async-start | bytes 8388608 | tf_op jit(solution)/shard_map/all_to_all | solution.py:28
  295.0 0.0 copy-done.2
  295.0 143.8 %all-gather = s32[32,2,2]{2,1,0:T(2,128)S(1)} all-gather(s32[1,2,2]{2,1,0:T(2,128)S(1)} %bitcast.20), channel_id=1, replica_groups=mesh['fsdp'=32,'tensor'=8] {'fsdp'}, dimensions={0}, use_global_device_ids=true | all-gather | bytes 528 | tf_op jit(solution)/shard_map/all_gather | solution.py:33
  438.8 0.1 copy.13
  438.9 0.1 copy.16
  439.0 0.0 all-to-all-done
  439.0 2.2 mul.46
  441.3 13.6 %fusion.5 = bf16[1536,256]{1,0:T(8,128)(2,1)} fusion(bf16[1536,8192]{1,0:T(8,128)(2,1)} %all-gather.3.cloned.1.call-done, bf16[8192,256]{1,0:T(8,128)(2,1)} %bitcast, bf16[1024,8,2,128]{3,2,1,0:T(2,128)(2,1)S(1)} %bitcast.17), kind=kOutput, calls=%fused_computation.8 | convolution fusion | flops 6444941312 | bytes 34340864 | tf_op jit(solution)/shard_map/dot_general | solution.py:24
  454.9 14.6 %reduce-scatter.2.cloned.1.call-done = f32[256,256]{1,0:T(8,128)} async-done(((f32[8192,256]{1,0:T(8,128)}), f32[256,256]{1,0:T(8,128)}) %reduce-scatter.2.cloned.1.call-update) | async-done | bytes 262160 | tf_op jit(solution)/shard_map/reduce_scatter | solution.py:39
  469.4 0.1 mul.49
  469.6 1.7 bitcast_multiply_fusion.4
  (3 shorter events, 0.0 us)
Async XLA Ops:
  7.2 260.6 %copy-start = (bf16[1536,256]{1,0:T(8,128)(2,1)S(1)}, bf16[1536,256]{1,0:T(8,128)(2,1)}, u32[]{:S(2)}) copy-start(bf16[1536,256]{1,0:T(8,128)(2,1)} %param.9) | copy-start | bytes 2359300
  7.2 260.6 %all-gather.3.cloned.1.call-start = ((), (), s32[]{:S(2)}) async-start(), calls=%async_computation.2 | async-start | bytes 28311552 | tf_op jit(solution)/shard_map/all_gather | solution.py:22
  15.1 454.3 %reduce-scatter.2.cloned.1.call-start = ((), (), s32[]{:S(2)}) async-start(), calls=%async_computation.3 | async-start | bytes 8650752 | tf_op jit(solution)/shard_map/reduce_scatter | solution.py:39
  281.7 0.9 copy-start.1
  282.6 12.4 %copy-start.2 = (s32[2,2]{1,0:T(2,128)S(1)}, s32[2,2]{1,0:T(2,128)}, u32[]{:S(2)}) copy-start(s32[2,2]{1,0:T(2,128)} %param.8) | copy-start | bytes 52
  285.0 154.0 %all-to-all-start = ((bf16[32,256,256]{2,1,0:T(8,128)(2,1)}), bf16[32,256,256]{2,1,0:T(8,128)(2,1)}, u32[]{:S(2)}, u32[]{:S(2)}) async-start(bf16[32,256,256]{2,1,0:T(8,128)(2,1)} %stack.2), calls=%async_computation | async-start | bytes 8388608 | tf_op jit(solution)/shard_map/all_to_all | solution.py:28
Sparse Core Ops, SparseCore 0:
  15.2 252.4 all-gather.2
  281.8 187.5 reduce-scatter.1
